TPU v7x, 256 devices: a whole 4x4x8 slice. The times are simulated.
256 devices in a mesh: seq: 128 (over x_lo, z, y, core), mp: 2 (over x_hi).
Axes of the slice: x: 4 (x_hi: 2, x_lo: 2; x = x_hi * 2 + x_lo), y: 4, z: 8, core: 2. Of those that a mesh axis runs over, the one named last changes fastest.
Arguments:
- patches: bfloat16 [32768, 64], P('seq'), may hold values from -6 to 6
- clip_shape: int32 [64, 3], replicated, may hold values from 1 to 16, as said below
- shard_counts: int32 [128], replicated, may hold values from 1 to 256, as said below
- patch_weight: bfloat16 [64, 2560], P(None, 'mp'), may hold values from -3 to 3
- patch_bias: float32 [2560], P('mp'), may hold values from -6 to 6
- time_mod: float32 [64, 2, 2560], P(None, None, 'mp'), may hold values from -6 to 6
- block_mod: float32 [2, 2560], P(None, 'mp'), may hold values from -4 to 4
- w_query: bfloat16 [2560, 2560], P('seq', 'mp'), may hold values from -0.47434165 to 0.47434165
- query_bias: float32 [2560], P('mp'), may hold values from -4 to 4
- w_keyvalue: bfloat16 [2560, 5120], P('seq', 'mp'), may hold values from -0.47434165 to 0.47434165
- keyvalue_bias: float32 [5120], P('mp'), may hold values from -6 to 6
- norm_gain: float32 [2, 2560], P(None, 'mp'), may hold values from 1 to 2
Outputs:
- attention: bfloat16 [32768, 2560], P('seq', 'mp')
Inputs may be any that keep to these rules, and one draw needn't show every extreme that they name: `clip_shape`: clip c lies on shards 2 c to 2 c + 1. Frames run from 1 to 2, patch rows from 8 to 16, patch columns from 8 to 16; some clip has 2 frames of 16 by 16 patches. `shard_counts`: the counts of clip c's 2 shards add up to the product of clip_shape[c].
All inputs are finite; a program needn't handle non-finite values.
Results may differ from a plain program's by a relative error of at most 0.0063.
Values may be sent and summed in bfloat16 or wider, within the bound.
A program may use at most 128 MiB of HBM per device.

v0:
```python
import math
import jax
import jax.numpy as jnp
from jax import lax
from jax.sharding import PartitionSpec as P

D = 2560
HEADS = 20
HD = 128
GROUP = 2
EPSILON = 1e-06


def partner_2(value, axis, apart):
    mask = 2**apart
    pairs = [(source, source ^ mask) for source in range(lax.axis_size(axis))]
    return lax.ppermute(value, axis, pairs)


def token_places(group_counts, member_ids, slot_ids, shape_row):
    before = jnp.cumsum(group_counts) - group_counts
    lookup = jnp.arange(GROUP, dtype=jnp.int32)[None, :] == member_ids[:, None]
    offset = jnp.sum(jnp.where(lookup, before[None, :], 0), axis=1)
    holding = jnp.sum(jnp.where(lookup, group_counts[None, :], 0), axis=1)
    position = offset + slot_ids
    plane_size = shape_row[1] * shape_row[2]
    frame_pos = position // plane_size
    row_pos = position // shape_row[2] % shape_row[1]
    col_pos = position % shape_row[2]
    return (slot_ids < holding, frame_pos, row_pos, col_pos)


def rotary_tables(frame_pos, row_pos, col_pos):
    other_pairs = HD // 6
    frame_pairs = HD // 2 - 2 * other_pairs
    pair_id = jnp.arange(HD, dtype=jnp.int32) // 2
    in_frame = pair_id < frame_pairs
    in_row = jnp.logical_and(pair_id >= frame_pairs, pair_id < frame_pairs + other_pairs)
    within = jnp.where(
        in_frame,
        pair_id,
        jnp.where(in_row, pair_id - frame_pairs, pair_id - frame_pairs - other_pairs),
    ).astype(jnp.float32)
    axis_span = jnp.where(in_frame, 2.0 * frame_pairs, 2.0 * other_pairs).astype(jnp.float32)
    inverse = jnp.exp(-(2.0 * within / axis_span) * math.log(10000.0))
    position = jnp.where(
        in_frame[None, :],
        frame_pos[:, None],
        jnp.where(in_row[None, :], row_pos[:, None], col_pos[:, None]),
    ).astype(jnp.float32)
    angles = position * inverse[None, :]
    return (jnp.cos(angles), jnp.sin(angles))


def rotate_pairs(values, cosine_table, sine_table):
    parity = jnp.arange(HD, dtype=jnp.int32) % 2 == 0
    partner = jnp.where(parity, -jnp.roll(values, -1, axis=-1), jnp.roll(values, 1, axis=-1))
    return values * cosine_table[:, None, :] + partner * sine_table[:, None, :]


def modulate_rows(embedded, row_sums, squares, modulation):
    average = row_sums / D
    variance = squares / D - average * average
    normed = (embedded - average[:, None]) * lax.rsqrt(variance[:, None] + EPSILON)
    return (normed * (1.0 + modulation[1]) + modulation[0]).astype(jnp.bfloat16)


def finish_heads(raw_rows, squares, scale_gain, cosine_table, sine_table):
    normed = raw_rows * lax.rsqrt(squares[:, None] / (HEADS * HD) + EPSILON) * scale_gain
    return rotate_pairs(normed.reshape(raw_rows.shape[0], -1, HD), cosine_table, sine_table).astype(
        jnp.bfloat16
    )


def contract(left_rows, pieces):
    return jnp.dot(left_rows, pieces, preferred_element_type=jnp.float32)


def split_pairs(pair_acc, keyvalue_bias, heads_here):
    tokens = pair_acc.shape[0]
    pair_raw = (pair_acc + keyvalue_bias).reshape(tokens, heads_here, 2, HD)
    key_raw = pair_raw[:, :, 0].reshape(tokens, heads_here * HD)
    value_rows = pair_raw[:, :, 1].reshape(tokens, heads_here * HD).astype(jnp.bfloat16)
    return (key_raw, value_rows)


def count_of(group_counts, source):
    return jnp.sum(jnp.where(jnp.arange(GROUP, dtype=jnp.int32) == source, group_counts, 0))


def gather_group(key_rows, value_rows, member):
    tokens = value_rows.shape[0]
    blocks = jnp.stack([key_rows.reshape(tokens, -1), value_rows])
    sources = [member]
    partner = partner_2(blocks, "seq", 0)
    blocks = jnp.concatenate([blocks, partner], axis=1)
    sources = sources + [jnp.bitwise_xor(source, 1 << 0) for source in sources]
    return (blocks, sources)


def attend_rows(queries, all_keys, all_values, key_valid):
    scores = jnp.einsum(
        "qhd,khd->hqk", queries, all_keys, preferred_element_type=jnp.float32
    ) * HD ** (-0.5)
    weights = jnp.where(key_valid[None, None, :], jnp.exp(scores), 0.0)
    totals = jnp.sum(weights, axis=-1)
    numerator = jnp.einsum(
        "hqk,khd->qhd", weights.astype(jnp.bfloat16), all_values, preferred_element_type=jnp.float32
    )
    return numerator / jnp.transpose(totals)[:, :, None]


def shards(
    patches,
    clip_shape,
    shard_counts,
    patch_weight,
    patch_bias,
    time_mod,
    block_mod,
    w_query,
    query_bias,
    w_keyvalue,
    keyvalue_bias,
    norm_gain,
):
    tokens = patches.shape[0]
    heads_here = w_query.shape[1] // HD
    seq_index = lax.axis_index("seq")
    clip_id = seq_index // GROUP
    member = seq_index % GROUP
    group_counts = lax.dynamic_slice_in_dim(shard_counts, clip_id * GROUP, GROUP, 0)
    shape_row = lax.dynamic_index_in_dim(clip_shape, clip_id, 0, keepdims=False)
    slot_ids = jnp.arange(tokens, dtype=jnp.int32)
    is_valid, frame_pos, row_pos, col_pos = token_places(
        group_counts, jnp.full((tokens,), member, jnp.int32), slot_ids, shape_row
    )
    modulation = lax.dynamic_index_in_dim(time_mod, clip_id, 0, keepdims=False) + block_mod
    embedded = jnp.dot(patches, patch_weight, preferred_element_type=jnp.float32) + patch_bias
    row_sums, squares = lax.psum(
        (jnp.sum(embedded, axis=1), jnp.sum(embedded * embedded, axis=1)), "mp"
    )
    half_rows = modulate_rows(embedded, row_sums, squares, modulation)
    hidden = lax.all_gather(half_rows, "mp", axis=1, tiled=True)
    cosine_table, sine_table = rotary_tables(frame_pos, row_pos, col_pos)
    query_acc = contract(hidden, lax.all_gather(w_query, "seq", axis=0, tiled=True))
    pair_acc = contract(hidden, lax.all_gather(w_keyvalue, "seq", axis=0, tiled=True))
    query_raw = query_acc + query_bias
    key_raw, value_rows = split_pairs(pair_acc, keyvalue_bias, heads_here)
    query_squares, key_squares = lax.psum(
        (jnp.sum(query_raw * query_raw, axis=1), jnp.sum(key_raw * key_raw, axis=1)), "mp"
    )
    queries = finish_heads(query_raw, query_squares, norm_gain[0], cosine_table, sine_table)
    key_rows = finish_heads(key_raw, key_squares, norm_gain[1], cosine_table, sine_table)
    blocks, sources = gather_group(key_rows, value_rows, member)
    key_valid = jnp.concatenate([slot_ids < count_of(group_counts, source) for source in sources])
    all_keys = blocks[0].reshape(-1, heads_here, HD)
    all_values = blocks[1].reshape(-1, heads_here, HD)
    result = attend_rows(queries, all_keys, all_values, key_valid)
    result = jnp.where(is_valid[:, None, None], result, 0.0)
    return result.reshape(tokens, heads_here * HD).astype(jnp.bfloat16)


def solution(mesh):
    return jax.shard_map(
        shards,
        mesh=mesh,
        in_specs=(
            P("seq", None),
            P(),
            P(),
            P(None, "mp"),
            P("mp"),
            P(None, None, "mp"),
            P(None, "mp"),
            P("seq", "mp"),
            P("mp"),
            P("seq", "mp"),
            P("mp"),
            P(None, "mp"),
        ),
        out_specs=P("seq", "mp"),
        check_vma=False,
    )
```

profile of v0, /device:TPU:1, one launch (start us, length us, event | category | flops | bytes accessed | tf_op | source)
XLA Modules:
  0.0 569.0 jit_solution(236258735546962702)
XLA Ops:
  6.5 0.0 copy-start
  6.5 0.0 all-gather.10.cloned.1.call-start
  6.5 0.7 all-gather.10.cloned.1.call-update
  7.3 0.0 all-gather.6.cloned.1.call-start
  7.3 0.1 copy-done
  7.5 1.2 fusion.33
  8.7 5.9 %all-reduce.1 = (f32[256]{0:T(256)S(1)}, f32[256]{0:T(256)S(1)}) all-reduce(f32[256]{0:T(256)S(1)} %get-tuple-element.6, f32[256]{0:T(256)S(1)} %get-tuple-element.5), channel_id=1, replica_groups=mesh['seq'=128,'mp'=2] {'mp'}, use_global_device_ids=true, to_apply=%region_4.5 | all-reduce | flops 512 | bytes 4096 | tf_op jit(solution)/shard_map/psum | solution.py:140
  14.6 0.0 copy-done.7
  14.6 0.7 bitcast_add_fusion
  15.3 0.0 copy-start.9
  15.3 0.0 copy-start.10
  15.4 0.0 copy-start.8
  15.4 1.1 add_convert_fusion
  16.5 0.0 all-gather.6.cloned.1.call-update
  16.5 0.0 all-gather.8.cloned.1.call-start
  16.6 0.7 all-gather.8.cloned.1.call-update
  17.3 0.0 copy-done.9
  17.3 0.1 constant_dynamic-slice_fusion
  17.4 0.6 fusion.39
  21.0 0.0 copy-done.10
  21.1 0.8 select_reduce_fusion.2
  21.8 0.2 reduce-window.9
  23.3 1.3 iota_compare_fusion
  24.7 0.1 select_reduce_fusion.1
  24.8 0.8 and_select_fusion.4
  25.6 0.6 fusion.26
  26.1 0.0 copy-start.12
  26.2 205.1 %all-gather.10.cloned.1.call-done = bf16[128,20,1280]{2,1,0:T(8,128)(2,1)} async-done(((bf16[1,20,1280]{2,1,0:T(8,128)(2,1)}), bf16[128,20,1280]{2,1,0:T(8,128)(2,1)}) %all-gather.10.cloned.1.call-update) | async-done | bytes 6553616 | tf_op jit(solution)/shard_map/all_gather | solution.py:146
  231.3 10.6 %reshape.424 = bf16[2560,1280]{1,0:T(8,128)(2,1)} reshape(bf16[128,20,1280]{2,1,0:T(8,128)(2,1)} %all-gather.10.cloned.1.call-done) | data formatting | bytes 13107200
  241.9 20.6 %all-gather.6.cloned.1.call-done = bf16[256,2560]{1,0:T(8,128)(2,1)} async-done(((bf16[256,1280]{1,0:T(8,128)(2,1)}), bf16[256,2560]{1,0:T(8,128)(2,1)}) %all-gather.6.cloned.1.call-update) | async-done | bytes 1310736 | tf_op jit(solution)/shard_map/all_gather | solution.py:144
  262.6 6.2 %multiply_reduce_fusion = (f32[256]{0:T(256)S(1)}, f32[256,1280]{1,0:T(8,128)}) fusion(f32[1280]{0:T(1024)S(1)} %copy-done.12, bf16[256,2560]{1,0:T(8,128)(2,1)} %all-gather.6.cloned.1.call-done, bf16[2560,1280]{1,0:T(8,128)(2,1)} %reshape.424), kind=kOutput, calls=%fused_computation.31 | convolution fusion | flops 1678704384 | bytes 9181184 | tf_op jit(solution)/shard_map/dot_general | solution.py:76
  268.7 222.9 %all-gather.8.cloned.1.call-done = bf16[128,20,2560]{2,1,0:T(8,128)(2,1)} async-done(((bf16[1,20,2560]{2,1,0:T(8,128)(2,1)}), bf16[128,20,2560]{2,1,0:T(8,128)(2,1)}) %all-gather.8.cloned.1.call-update) | async-done | bytes 13107216 | tf_op jit(solution)/shard_map/all_gather | solution.py:147
  491.7 18.0 %reshape.422 = bf16[2560,2560]{1,0:T(8,128)(2,1)} reshape(bf16[128,20,2560]{2,1,0:T(8,128)(2,1)} %all-gather.8.cloned.1.call-done) | data formatting | bytes 26214400
  509.7 0.0 copy-done.11
  509.7 7.0 %convolution_add_fusion = f32[256,2560]{1,0:T(8,128)S(1)} fusion(bf16[256,2560]{1,0:T(8,128)(2,1)} %all-gather.6.cloned.1.call-done, bf16[2560,2560]{1,0:T(8,128)(2,1)} %reshape.422, f32[2560]{0:T(1024)S(1)} %copy-done.11), kind=kOutput, calls=%fused_computation.3 | convolution fusion | flops 3356098560 | bytes 17049600 | tf_op jit(solution)/shard_map/dot_general | solution.py:76
  516.7 2.8 reshape.417
  519.5 2.6 slice.84
  522.1 0.2 multiply_reduce_fusion.1
  522.3 5.5 all-reduce
  527.8 0.2 fusion.16
  528.0 1.5 fusion.37
  529.5 2.0 fusion.38
  531.5 2.1 copy.42
  533.6 4.3 slice.89
  538.0 1.5 maximum_negate_fusion
  539.5 2.9 copy.43
  542.3 1.5 pad_maximum_fusion.1
  543.9 2.9 copy.44
  546.8 0.0 copy-done.3
  546.8 1.0 copy.54
  547.7 2.5 fusion.15
  550.3 0.0 copy-start.6
  550.3 1.2 pad_maximum_fusion.2
  551.5 2.3 collective-permute-start
  553.7 1.3 multiply_multiply_fusion
  555.0 1.7 copy.46
  556.7 0.3 fusion.36
  557.0 0.0 collective-permute-done
  557.0 1.5 pad_maximum_fusion
  558.5 0.2 fusion.34
  558.7 1.6 fusion
  560.3 0.0 copy-start.1
  560.4 1.0 select_convert_fusion
  561.4 1.1 copy.49
  (26 shorter events, 0.2 us)
Async XLA Ops:
  6.5 0.9 copy-start
  6.5 8.0 %copy-start.7 = (f32[2,1280]{1,0:T(2,128)S(1)}, f32[2,1280]{1,0:T(2,128)}, u32[]{:S(2)}) copy-start(f32[2,1280]{1,0:T(2,128)} %param.18) | copy-start | bytes 30724
  6.5 224.8 %all-gather.10.cloned.1.call-start = ((), (), s32[]{:S(2)}) async-start(), calls=%async_computation.2 | async-start | bytes 7925760 | tf_op jit(solution)/shard_map/all_gather | solution.py:146
  7.3 255.3 %all-gather.6.cloned.1.call-start = ((), (), s32[]{:S(2)}) async-start(), calls=%async_computation | async-start | bytes 1966080 | tf_op jit(solution)/shard_map/all_gather | solution.py:144
  15.3 1.9 copy-start.9
  15.3 5.7 %copy-start.10 = (s32[128]{0:T(128)S(1)}, s32[128]{0:T(128)}, u32[]{:S(2)}) copy-start(s32[128]{0:T(128)} %param.14) | copy-start | bytes 1540
  15.4 9.2 %copy-start.8 = (f32[2,1280]{1,0:T(2,128)S(1)}, f32[2,1280]{1,0:T(2,128)}, u32[]{:S(2)}) copy-start(f32[2,1280]{1,0:T(2,128)} %param.23) | copy-start | bytes 30724
  16.5 475.1 %all-gather.8.cloned.1.call-start = ((), (), s32[]{:S(2)}) async-start(), calls=%async_computation.1 | async-start | bytes 15851520 | tf_op jit(solution)/shard_map/all_gather | solution.py:147
  26.1 236.4 %copy-start.12 = (f32[1280]{0:T(1024)S(1)}, f32[1280]{0:T(1024)}, u32[]{:S(2)}) copy-start(f32[1280]{0:T(1024)} %param.20) | copy-start | bytes 15364
  268.7 241.0 %copy-start.11 = (f32[2560]{0:T(1024)S(1)}, f32[2560]{0:T(1024)}, u32[]{:S(2)}) copy-start(f32[2560]{0:T(1024)} %param.22) | copy-start | bytes 30724
  533.6 4.3 copy-start.4
  533.6 4.3 copy-start.5
  539.5 2.9 copy-start.2
  543.9 2.9 copy-start.3
  550.3 3.5 copy-start.6
  551.5 5.6 collective-permute-start
  560.3 2.1 copy-start.1
Sparse Core Ops, SparseCore 0:
  9.2 222.0 all-gather.9
  233.1 29.4 all-gather.5
  264.4 227.1 all-gather.7
where the time goes:
time: 570 us; the launch traced here: 569 us
  waiting for transfers between devices  450 us (79%)
  local copies, waits for them, and re-layouts  55 us (10%)
  between operations  17.7 us (3%)
  matrix products  17.1 us (3%)
  other arithmetic  15.4 us (3%)
  blocking collectives  11.3 us (2%)
    all_gather x1, waiting for transfers between devices, shards(): lax.all_gather(w_keyvalue, 'seq', axis=0, tiled=True)  223 us
    all_gather x1, waiting for transfers between devices, shards(): lax.all_gather(w_query, 'seq', axis=0, tiled=True)  205 us
    unnamed x29, local copies, waits for them, and re-layouts  29.8 us
    all_gather x1, waiting for transfers between devices, shards(): hidden = lax.all_gather(half_rows, 'mp', axis=1, tiled=True)  20.6 us
    dot_general x2, matrix products, contract(): return jnp.dot(left_rows, pieces, preferred_element_type=jnp.float32)  13.2 us
  transfers between devices with their start and end apart: 4, of which 3 were waited for; matrix products, arithmetic and copies ran while one was open for 5% of the time, Pallas kernels for 0%

commit v1 on v0

--- a/solution.py
+++ b/solution.py
@@ -143,7 +143,12 @@
     half_rows = modulate_rows(embedded, row_sums, squares, modulation)
     hidden = lax.all_gather(half_rows, "mp", axis=1, tiled=True)
     cosine_table, sine_table = rotary_tables(frame_pos, row_pos, col_pos)
-    query_acc = contract(hidden, lax.all_gather(w_query, "seq", axis=0, tiled=True))
+    query_acc = contract(
+        hidden,
+        jnp.concatenate(
+            lax.all_to_all(jnp.stack([w_query] * lax.axis_size("seq")), "seq", 0, 0), axis=0
+        ),
+    )
     pair_acc = contract(hidden, lax.all_gather(w_keyvalue, "seq", axis=0, tiled=True))
     query_raw = query_acc + query_bias
     key_raw, value_rows = split_pairs(pair_acc, keyvalue_bias, heads_here)

time: 570 us -> 456 us (0.80)
  waiting for transfers between devices: 450 us -> 312 us
  starting transfers between devices: 2.35 us -> 18.3 us
    all_gather x1 -> x0, waiting for transfers between devices: 205 us -> none  [shards(): lax.all_gather(w_query, 'seq', axis=0, tiled=True)]
    all_to_all x0 -> x1, waiting for transfers between devices: none -> 194 us  [shards(): lax.all_to_all(jnp.stack([w_query] * lax.axis_size('seq')), 'seq', 0, 0)]
    all_gather x1, waiting for transfers between devices: 223 us -> 118 us  [shards(): lax.all_gather(w_keyvalue, 'seq', axis=0, tiled=True)]
    all_gather x1, waiting for transfers between devices: 20.6 us -> 0.01 us  [shards(): hidden = lax.all_gather(half_rows, 'mp', axis=1, tiled=True)]
    all_to_all x0 -> x1, starting transfers between devices: none -> 16 us  [shards(): lax.all_to_all(jnp.stack([w_query] * lax.axis_size('seq')), 'seq', 0, 0)]
    reshape x0 -> x1, local copies, waits for them, and re-layouts: none -> 10.6 us  [shards(): jnp.concatenate(lax.all_to_all(jnp.stack([w_query] * lax.axis_size('seq')...]
    unnamed x29 -> x28, local copies, waits for them, and re-layouts: 29.8 us -> 19.2 us
  transfers between devices with their start and end apart: 4 -> 4, of which waited for: 3 -> 2; matrix products, arithmetic and copies ran while one was open for 5% -> 6% of each run, Pallas kernels for 0% -> 0%
where the time goes in v1:
time: 456 us; the launch traced here: 453 us
  waiting for transfers between devices  312 us (68%)
  local copies, waits for them, and re-layouts  57.4 us (13%)
  starting transfers between devices  18.3 us (4%)
  other arithmetic  18.3 us (4%)
  between operations  17.8 us (4%)
  matrix products  17.1 us (4%)
  blocking collectives  11.3 us (2%)
    all_to_all x1, waiting for transfers between devices, shards(): lax.all_to_all(jnp.stack([w_query] * lax.axis_size('seq')), 'seq', 0, 0)  194 us
    all_gather x1, waiting for transfers between devices, shards(): lax.all_gather(w_keyvalue, 'seq', axis=0, tiled=True)  118 us
    unnamed x28, local copies, waits for them, and re-layouts  19.2 us
    all_to_all x1, starting transfers between devices, shards(): lax.all_to_all(jnp.stack([w_query] * lax.axis_size('seq')), 'seq', 0, 0)  16 us
    dot_general x2, matrix products, contract(): return jnp.dot(left_rows, pieces, preferred_element_type=jnp.float32)  13.2 us
    reshape x1, local copies, waits for them, and re-layouts, shards(): jnp.concatenate(lax.all_to_all(jnp.stack([w_query] * lax.axis_size('seq')...  10.6 us
  transfers between devices with their start and end apart: 4, of which 2 were waited for; matrix products, arithmetic and copies ran while one was open for 6% of the time, Pallas kernels for 0%

profile of v1, /device:TPU:1, one launch (start us, length us, event | category | flops | bytes accessed | tf_op | source)
XLA Modules:
  0.0 452.6 jit_solution(13002182191155310422)
XLA Ops:
  6.5 0.0 copy-start
  6.5 0.0 all-gather.4.cloned.1.call-start
  6.5 0.8 bitcast_add_fusion
  7.3 0.1 copy-done
  7.5 1.2 fusion.33
  8.7 5.9 %all-reduce.1 = (f32[256]{0:T(256)S(1)}, f32[256]{0:T(256)S(1)}) all-reduce(f32[256]{0:T(256)S(1)} %get-tuple-element.6, f32[256]{0:T(256)S(1)} %get-tuple-element.5), channel_id=1, replica_groups=mesh['seq'=128,'mp'=2] {'mp'}, use_global_device_ids=true, to_apply=%region_4.5 | all-reduce | flops 512 | bytes 4096 | tf_op jit(solution)/shard_map/psum | solution.py:140
  14.6 1.1 add_convert_fusion
  15.7 0.0 all-gather.4.cloned.1.call-update
  15.8 0.0 all-gather.6.cloned.1.call-start
  15.8 0.7 all-gather.6.cloned.1.call-update
  16.5 0.0 copy-done.7
  16.5 3.7 stack.5
  20.2 16.0 %all-to-all-start = ((bf16[128,20,1280]{2,1,0:T(8,128)(2,1)}), bf16[128,20,1280]{2,1,0:T(8,128)(2,1)}, u32[]{:S(2)}, u32[]{:S(2)}) async-start(bf16[128,20,1280]{2,1,0:T(8,128)(2,1)} %stack.5), calls=%async_computation | async-start | bytes 15728640 | tf_op jit(solution)/shard_map/all_to_all | solution.py:149
  36.2 0.0 copy-done.9
  36.2 0.1 constant_dynamic-slice_fusion
  36.3 0.5 fusion.39
  39.8 0.0 copy-done.10
  39.8 0.8 select_reduce_fusion.2
  40.6 0.2 reduce-window.9
  42.0 1.4 iota_compare_fusion
  43.4 0.0 copy-done.8
  43.4 0.1 select_reduce_fusion.1
  43.5 0.8 and_select_fusion.4
  44.3 0.6 fusion.26
  44.9 0.0 copy-start.12
  44.9 193.6 %all-to-all-done = bf16[128,20,1280]{2,1,0:T(8,128)(2,1)} async-done(((bf16[128,20,1280]{2,1,0:T(8,128)(2,1)}), bf16[128,20,1280]{2,1,0:T(8,128)(2,1)}, u32[]{:S(2)}, u32[]{:S(2)}) %all-to-all-start) | async-done | bytes 6553632 | tf_op jit(solution)/shard_map/all_to_all | solution.py:149
  238.6 10.6 %reshape.425 = bf16[2560,1280]{1,0:T(8,128)(2,1)} reshape(bf16[128,20,1280]{2,1,0:T(8,128)(2,1)} %all-to-all-done) | data formatting | bytes 13107200 | tf_op jit(solution)/shard_map/reshape | solution.py:148
  249.2 0.0 copy-done.12
  249.2 6.2 %multiply_reduce_fusion = (f32[256]{0:T(256)S(1)}, f32[256,1280]{1,0:T(8,128)}) fusion(f32[1280]{0:T(1024)S(1)} %copy-done.12, bf16[256,2560]{1,0:T(8,128)(2,1)} %all-gather.4.cloned.1.call-done, bf16[2560,1280]{1,0:T(8,128)(2,1)} %reshape.425), kind=kOutput, calls=%fused_computation.31 | convolution fusion | flops 1678704384 | bytes 9181184 | tf_op jit(solution)/shard_map/dot_general | solution.py:76
  255.5 118.0 %all-gather.6.cloned.1.call-done = bf16[128,20,2560]{2,1,0:T(8,128)(2,1)} async-done(((bf16[1,20,2560]{2,1,0:T(8,128)(2,1)}), bf16[128,20,2560]{2,1,0:T(8,128)(2,1)}) %all-gather.6.cloned.1.call-update) | async-done | bytes 13107216 | tf_op jit(solution)/shard_map/all_gather | solution.py:152
  373.5 18.0 %reshape.428 = bf16[2560,2560]{1,0:T(8,128)(2,1)} reshape(bf16[128,20,2560]{2,1,0:T(8,128)(2,1)} %all-gather.6.cloned.1.call-done) | data formatting | bytes 26214400
  391.5 0.0 copy-done.11
  391.5 7.0 %convolution_add_fusion = f32[256,2560]{1,0:T(8,128)S(1)} fusion(bf16[256,2560]{1,0:T(8,128)(2,1)} %all-gather.4.cloned.1.call-done, bf16[2560,2560]{1,0:T(8,128)(2,1)} %reshape.428, f32[2560]{0:T(1024)S(1)} %copy-done.11), kind=kOutput, calls=%fused_computation.3 | convolution fusion | flops 3356098560 | bytes 17049600 | tf_op jit(solution)/shard_map/dot_general | solution.py:76
  398.5 2.8 reshape.422
  401.3 2.8 slice.84
  404.1 0.0 copy-done.2
  404.1 2.4 slice.89
  406.6 0.2 multiply_reduce_fusion.1
  406.8 2.2 copy.42
  408.9 5.4 %all-reduce = (f32[256]{0:T(256)S(1)}, f32[256]{0:T(256)S(1)}) all-reduce(f32[256]{0:T(256)S(1)} %multiply_reduce_fusion.1, f32[256]{0:T(256)S(1)} %get-tuple-element.40), channel_id=1, replica_groups=mesh['seq'=128,'mp'=2] {'mp'}, use_global_device_ids=true, to_apply=%region_6.7 | all-reduce | flops 512 | bytes 4096 | tf_op jit(solution)/shard_map/psum | solution.py:155
  414.4 0.2 fusion.16
  414.6 2.0 fusion.38
  416.6 1.9 fusion.37
  418.5 0.0 copy-done.3
  418.5 1.0 copy.54
  419.5 3.3 maximum_negate_fusion
  422.8 2.9 copy.43
  425.7 0.0 copy-done.4
  425.7 2.8 pad_maximum_fusion.1
  428.5 2.9 copy.44
  431.4 2.1 fusion.15
  433.5 0.0 copy-start.6
  433.6 1.2 pad_maximum_fusion.2
  434.7 2.3 collective-permute-start
  437.0 1.3 multiply_multiply_fusion
  438.3 1.7 copy.46
  440.0 0.3 fusion.36
  440.3 0.0 collective-permute-done
  440.3 1.5 pad_maximum_fusion
  441.8 0.2 fusion.34
  442.0 1.6 fusion
  443.6 0.0 copy-start.1
  443.6 1.0 select_convert_fusion
  444.7 1.1 copy.49
  (26 shorter events, 0.2 us)
Async XLA Ops:
  6.5 0.9 copy-start
  6.5 242.7 %all-gather.4.cloned.1.call-start = ((), (), s32[]{:S(2)}) async-start(), calls=%async_computation.1 | async-start | bytes 1966080 | tf_op jit(solution)/shard_map/all_gather | solution.py:144
  14.6 1.9 copy-start.7
  15.8 357.7 %all-gather.6.cloned.1.call-start = ((), (), s32[]{:S(2)}) async-start(), calls=%async_computation.2 | async-start | bytes 15851520 | tf_op jit(solution)/shard_map/all_gather | solution.py:152
  20.2 16.0 %copy-start.9 = (s32[64,3]{0,1:T(4,128)S(1)}, s32[64,3]{0,1:T(4,128)}, u32[]{:S(2)}) copy-start(s32[64,3]{0,1:T(4,128)} %param.13) | copy-start | bytes 2308
  20.2 19.5 %copy-start.10 = (s32[128]{0:T(128)S(1)}, s32[128]{0:T(128)}, u32[]{:S(2)}) copy-start(s32[128]{0:T(128)} %param.14) | copy-start | bytes 1540
  20.2 23.2 %copy-start.8 = (f32[2,1280]{1,0:T(2,128)S(1)}, f32[2,1280]{1,0:T(2,128)}, u32[]{:S(2)}) copy-start(f32[2,1280]{1,0:T(2,128)} %param.23) | copy-start | bytes 30724
  20.2 218.3 %all-to-all-start = ((bf16[128,20,1280]{2,1,0:T(8,128)(2,1)}), bf16[128,20,1280]{2,1,0:T(8,128)(2,1)}, u32[]{:S(2)}, u32[]{:S(2)}) async-start(bf16[128,20,1280]{2,1,0:T(8,128)(2,1)} %stack.5), calls=%async_computation | async-start | bytes 15728640 | tf_op jit(solution)/shard_map/all_to_all | solution.py:149
  44.9 204.3 %copy-start.12 = (f32[1280]{0:T(1024)S(1)}, f32[1280]{0:T(1024)}, u32[]{:S(2)}) copy-start(f32[1280]{0:T(1024)} %param.20) | copy-start | bytes 15364
  255.5 136.1 %copy-start.11 = (f32[2560]{0:T(1024)S(1)}, f32[2560]{0:T(1024)}, u32[]{:S(2)}) copy-start(f32[2560]{0:T(1024)} %param.22) | copy-start | bytes 30724
  401.3 2.8 copy-start.2
  416.6 1.9 copy-start.3
  422.8 2.9 copy-start.4
  428.5 2.9 copy-start.5
  433.5 3.5 copy-start.6
  434.7 5.6 %collective-permute-start = (bf16[2,256,1280]{1,2,0:T(8,128)(2,1)}, bf16[2,256,1280]{1,2,0:T(8,128)(2,1)}, u32[]{:S(2)}, u32[]{:S(2)}) collective-permute-start(bf16[2,256,1280]{1,2,0:T(8,128)(2,1)} %pad_maximum_fusion.2), channel_id=1, source_target_pairs={{0,2},{2,0},{4,6},{6,4},{8,10},{10,8},{12,14},{14,12},{16,18},{18,... | collective-permute-start | bytes 3932168 | tf_op jit(solution)/shard_map/ppermute | solution.py:17
  443.6 2.1 copy-start.1
Sparse Core Ops, SparseCore 0:
  15.9 61.4 all-gather.3
  79.3 294.1 all-gather.5
